TPU v7x, 32 devices: a whole 2x2x4 slice. The times are simulated.
32 devices in a mesh: groups: 2 (over y), row: 4 (over z), col: 4 (over x, core).
Axes of the slice: x: 2, y: 2, z: 4, core: 2. Of those that a mesh axis runs over, the one named last changes fastest.
Arguments:
- raw_files: bfloat16 [128, 4, 8, 12000], P(('groups', 'row'), 'col'), parts along dimension 0
- file_channels: int32 [128, 4], P(('groups', 'row'), 'col'), parts along dimension 0, may hold values from 0 to 255, as said below
- reader_counts: int32 [8, 4], P(('groups', 'row'), 'col'), parts along dimension 0, may hold values from 0 to 16, as said below
- fir_taps: float32 [32], replicated, may hold values from -1 to 1
- band_bins: int32 [64], replicated, may hold values from 1 to 1499, as said below
Outputs:
- stack: bfloat16 [512, 4, 64, 128], P(('groups', 'row'), 'col'), parts along dimension 0
There are 2 independent parts, one for each index of `groups`. A program takes and returns all parts, laid end to end along the dimension named above; an argument that names none is the same for every part. Nothing has to cross between parts.
Inputs may be any that keep to these rules, and one draw needn't show every extreme that they name: `file_channels`: channel q belongs to owner row q // 64, column (q // 16) % 4. Every channel stands in exactly one live slot (slot below its reader's count), of a reader in its owner's column. Live slots of one reader name at most 4 channels of one owner; in every column some reader holds exactly 4 channels of every owner. Slots at or above the count hold arbitrary channel numbers. `reader_counts`: in every column some reader holds 16 live slots. `band_bins`: Distinct.
All inputs are finite; a program needn't handle non-finite values.
Results may differ from a plain program's by a relative error of at most 0.017.
Values may be sent and summed in bfloat16 or wider, within the bound.
No kernel may reach another device: no remote copies, remote signals or barrier semaphores. Data moves between devices by JAX's collectives and lax.ppermute only.
A program may use at most 64 MiB of HBM per device.

v0:
```python
import math
import jax
import jax.numpy as jnp
from jax import lax
from jax.sharding import PartitionSpec as P

CH_DEV = 16
DEC = 4


def decimate(signal, fir_taps):
    count, records, samples = signal.shape
    length = samples // DEC
    taps = fir_taps.shape[0]
    outputs = 128
    span = outputs * DEC
    blocks = (length + outputs - 1) // outputs
    total = (blocks + 1) * span
    padded = jnp.pad(signal, ((0, 0), (0, 0), (0, total - samples)))
    leading = padded[:, :, : blocks * span].reshape(count, records, blocks, span)
    following = padded[:, :, span:].reshape(count, records, blocks, span)[:, :, :, : taps - DEC]
    window = jnp.concatenate([leading, following], axis=3)
    positions = jnp.arange(span + taps - DEC, dtype=jnp.int32)[:, None]
    columns = jnp.arange(outputs, dtype=jnp.int32)[None, :]
    offset = positions - DEC * columns
    banded = jnp.zeros((span + taps - DEC, outputs), jnp.float32)
    for index in range(taps):
        banded = banded + jnp.where(offset == index, fir_taps[index], jnp.float32(0.0))
    upper = banded.astype(jnp.bfloat16)
    lower = (banded - upper.astype(jnp.float32)).astype(jnp.bfloat16)
    result = jnp.einsum("iqbw,wn->iqbn", window, upper, preferred_element_type=jnp.float32)
    result = result + jnp.einsum("iqbw,wn->iqbn", window, lower, preferred_element_type=jnp.float32)
    return result.reshape(count, records, blocks * outputs)[:, :, :length].astype(jnp.bfloat16)


def whiten(signal, fir_taps, band_bins):
    count, records, samples = signal.shape
    length = samples // DEC
    decimated = decimate(signal, fir_taps)
    steps = jnp.arange(length, dtype=jnp.int32)
    product = band_bins[None, :] * steps[:, None] % length
    angle = 2.0 * math.pi / length * product.astype(jnp.float32)
    table = jnp.concatenate([jnp.cos(angle), -jnp.sin(angle)], axis=1).astype(jnp.bfloat16)
    spectra = jnp.dot(
        decimated.reshape(count * records, length), table, preferred_element_type=jnp.float32
    )
    power = jnp.mean(spectra * spectra, axis=1, keepdims=True)
    white = spectra / jnp.sqrt(power + 1e-06)
    return white.reshape(count, records, table.shape[1]).astype(jnp.bfloat16)


def slot_plan(file_channels, reader_counts, nrows, ncols, capacity):
    channels = file_channels[:, 0]
    slots = channels.shape[0]
    order = jnp.arange(slots, dtype=jnp.int32)
    live = order < reader_counts[0, 0]
    owner = channels // (CH_DEV * ncols)
    place = channels % CH_DEV
    earlier = (owner[None, :] == owner[:, None]) & live[None, :] & (order[None, :] < order[:, None])
    rank = jnp.sum(earlier.astype(jnp.int32), axis=1)
    where_to = jnp.where(live, owner * capacity + rank, -1)
    target = jnp.arange(nrows * capacity, dtype=jnp.int32)
    match = (where_to[None, :] == target[:, None]).astype(jnp.int32)
    filled = jnp.sum(match, axis=1) > 0
    source = jnp.sum(match * order[None, :], axis=1)
    label = jnp.where(filled, jnp.sum(match * place[None, :], axis=1), -1)
    return (source, filled, label)


def pack(data, source, filled, nrows, capacity):
    chosen = jnp.where(filled[:, None, None], data[source], jnp.zeros((), data.dtype))
    return chosen.reshape((nrows, capacity) + data.shape[1:])


def settle(received, labels):
    flat = received.reshape((-1,) + received.shape[2:])
    marks = labels.reshape(-1).astype(jnp.int32)
    total = marks.shape[0]
    match = (marks[None, :] == jnp.arange(CH_DEV, dtype=jnp.int32)[:, None]).astype(jnp.int32)
    source = jnp.sum(match * jnp.arange(total, dtype=jnp.int32)[None, :], axis=1)
    return flat[source]


def on_device(raw_files, file_channels, reader_counts, fir_taps, band_bins):
    nrows = lax.axis_size("row")
    ncols = lax.axis_size("col")
    capacity = max(2, (CH_DEV + nrows - 1) // nrows)
    source, filled, label = slot_plan(file_channels, reader_counts, nrows, ncols, capacity)
    labels = label.reshape(nrows, capacity).astype(jnp.bfloat16)
    reader_white = whiten(raw_files[:, 0], fir_taps, band_bins)
    outgoing = pack(reader_white, source, filled, nrows, capacity)
    arrived, arrived_labels = (
        lax.all_to_all(outgoing, "row", split_axis=0, concat_axis=0, tiled=True),
        lax.all_to_all(labels, "row", split_axis=0, concat_axis=0, tiled=True),
    )
    white_own = settle(arrived, arrived_labels)
    records = white_own.shape[1]
    width = white_own.shape[2] // 2
    row_white = lax.all_gather(white_own, "col", axis=0, tiled=True)
    left_count = row_white.shape[0]
    left = (
        row_white.reshape(left_count, records, 2, width)
        .transpose(0, 2, 1, 3)
        .reshape(left_count, 2 * records, width)
    )
    piece = lax.all_gather(white_own, "row", axis=0, tiled=True)
    right_count = piece.shape[0]
    split_piece = piece.reshape(right_count, records, 2, width)
    piece_re = split_piece[:, :, 0, :]
    piece_im = split_piece[:, :, 1, :]
    right_real = jnp.concatenate([piece_re, piece_im], axis=1)
    right_imag = jnp.concatenate([-piece_im, piece_re], axis=1)
    real = jnp.einsum("ikb,jkb->ijb", left, right_real, preferred_element_type=jnp.float32)
    imag = jnp.einsum("ikb,jkb->ijb", left, right_imag, preferred_element_type=jnp.float32)
    stacked = (jnp.concatenate([real, imag], axis=2) / records).astype(jnp.bfloat16)
    return stacked[:, None, :, :]


def solution(mesh):
    return jax.shard_map(
        on_device,
        mesh=mesh,
        in_specs=(
            P(("groups", "row"), "col", None, None),
            P(("groups", "row"), "col"),
            P(("groups", "row"), "col"),
            P(),
            P(),
        ),
        out_specs=P(("groups", "row"), "col", None, None),
        check_vma=False,
    )
```

profile of v0, /device:TPU:0, one launch (start us, length us, event | category | flops | bytes accessed | tf_op | source)
XLA Modules:
  0.0 111.3 jit_solution(5888975628344206008)
XLA Ops:
  0.0 0.7 and_select_fusion.2
  0.7 0.7 fusion.64
  2.0 0.2 convert_reduce_fusion.1
  2.2 0.1 select_reduce_fusion.1
  2.3 0.7 convert_element_type.76
  3.0 6.3 %all-to-all-start.1 = ((bf16[4,1,4]{2,1,0:T(2,128)(2,1)}), bf16[4,1,4]{2,1,0:T(2,128)(2,1)S(1)}, u32[]{:S(2)}, u32[]{:S(2)}) async-start(bf16[4,1,4]{2,1,0:T(2,128)(2,1)} %convert_element_type.76), calls=%async_computation.1 | async-start | bytes 4096 | tf_op jit(solution)/shard_map/all_to_all | solution.py:94
  9.4 2.1 %fusion.137 = (f32[1]{0:T(128)}, f32[1]{0:T(128)}, f32[1]{0:T(128)}, f32[1]{0:T(128)}, f32[1]{0:T(128)}, /*index=5*/f32[1]{0:T(128)}, f32[1]{0:T(128)}, f32[1]{0...) fusion(f32[32]{0:T(128)} %param.8), kind=kLoop, calls=%fused_computation.186 | loop fusion | bytes 152 | tf_op jit(solution)/shard_map/slice | solution.py:28
  11.5 1.8 %fusion.138 = (f32[1]{0:T(128)}, f32[1]{0:T(128)}, f32[1]{0:T(128)}, f32[1]{0:T(128)}, f32[1]{0:T(128)}, /*index=5*/f32[1]{0:T(128)}, f32[1]{0:T(128)}, f32[1]{0...) fusion(f32[32]{0:T(128)} %param.8), kind=kLoop, calls=%fused_computation.187 | loop fusion | bytes 104 | tf_op jit(solution)/shard_map/slice | solution.py:28
  13.3 3.2 %pad_slice_fusion.1 = (bf16[16,8,12288]{2,1,0:T(8,128)(2,1)S(1)}, bf16[16,8,12288]{2,1,0:T(8,128)(2,1)S(1)}) fusion(bf16[16,8,12000]{2,1,0:T(8,128)(2,1)} %bitcast.115), kind=kLoop, calls=%fused_computation.6 | loop fusion | bytes 9363456 | tf_op jit(solution)/shard_map/slice | solution.py:20
  16.5 1.3 %copy.29 = bf16[16,8,24,512]{3,2,1,0:T(8,128)(2,1)S(1)} copy(bf16[16,8,24,512]{3,1,2,0:T(8,128)(2,1)S(1)} %bitcast.112) | data formatting | bytes 6291456
  17.8 0.1 slice.157
  17.9 1.3 %copy.30 = bf16[16,8,24,512]{3,2,1,0:T(8,128)(2,1)S(1)} copy(bf16[16,8,24,512]{3,1,2,0:T(8,128)(2,1)S(1)} %bitcast.111) | data formatting | bytes 6291456
  19.2 22.2 %fusion = f32[16,8,24,128]{3,2,1,0:T(8,128)S(1)} fusion(bf16[16,8,24,28]{3,2,1,0:T(8,128)(2,1)S(1)} %slice.157, bf16[16,8,24,512]{3,2,1,0:T(8,128)(2,1)S(1)} %copy.30, f32[]{:T(128)} %bitcast.35, f32[]{:T(128)} %bitcast.34, f32[]{:T(128)} %bitcast.33, f32[]{:T(128)} %bitcast.32, f32[]{:T(128)} %bitcast.31, f32[]{:T(128)} %bitcast.30, f32[]{:T(128)} %bitcast.29, ...), kind=kOutput, calls=%fused_computation.7 | convolution fusion | flops 438220800 | bytes 4891264 | tf_op jit(solution)/shard_map/iqbw,wn->iqbn/dot_general | solution.py:32
  41.4 0.0 copy-start
  41.4 22.0 %add_convert_fusion = bf16[16,8,24,128]{3,2,1,0:T(8,128)(2,1)S(1)} fusion(f32[16,8,24,128]{3,2,1,0:T(8,128)S(1)} %fusion, bf16[16,8,24,28]{3,2,1,0:T(8,128)(2,1)S(1)} %slice.157, bf16[16,8,24,512]{3,2,1,0:T(8,128)(2,1)S(1)} %copy.30, f32[]{:T(128)} %bitcast.35, f32[]{:T(128)} %bitcast.34, f32[]{:T(128)} %bitcast.33, f32[]{:T(128)} %bitcast.32, ...), kind=kOutput, calls=%fused_computation.11 | convolution fusion | flops 438799872 | bytes 5677696 | tf_op jit(solution)/shard_map/iqbw,wn->iqbn/dot_general | solution.py:31
  63.4 0.3 reshape.222
  63.7 0.0 copy-done
  63.8 3.6 %cosine_convert_fusion = (bf16[3000,64]{0,1:T(8,128)(2,1)S(1)}, bf16[3000,64]{0,1:T(8,128)(2,1)S(1)}) fusion(s32[64]{0:T(128)S(1)} %copy-done), kind=kLoop, calls=%fused_computation.21 | loop fusion | flops 2304000 | bytes 768256 | tf_op jit(solution)/shard_map/convert.1
  67.4 0.5 multiply_reduce_fusion
  67.9 0.1 gt.20
  67.9 0.1 fusion.60
  68.0 0.6 gather_fusion
  68.6 0.7 broadcast_select_fusion
  69.3 0.0 all-to-all-done.1
  69.3 5.1 %all-to-all-start = ((bf16[4,4,8,128]{3,2,1,0:T(8,128)(2,1)}), bf16[4,4,8,128]{3,2,1,0:T(8,128)(2,1)S(1)}, u32[]{:S(2)}, u32[]{:S(2)}) async-start(bf16[4,4,8,128]{3,2,1,0:T(8,128)(2,1)} %broadcast_select_fusion), calls=%async_computation | async-start | bytes 65536 | tf_op jit(solution)/shard_map/all_to_all | solution.py:93
  74.4 0.1 reshape.228
  74.5 0.1 select_reduce_fusion
  74.7 5.4 %all-to-all-done = bf16[4,4,8,128]{3,2,1,0:T(8,128)(2,1)S(1)} async-done(((bf16[4,4,8,128]{3,2,1,0:T(8,128)(2,1)}), bf16[4,4,8,128]{3,2,1,0:T(8,128)(2,1)S(1)}, u32[]{:S(2)}, u32[]{:S(2)}) %all-to-all-start) | async-done | bytes 32800 | tf_op jit(solution)/shard_map/all_to_all | solution.py:93
  80.1 0.6 gather_fusion.1
  80.6 13.3 %all-gather = bf16[64,8,128]{2,1,0:T(8,128)(2,1)S(1)} all-gather(bf16[16,8,128]{2,1,0:T(8,128)(2,1)S(1)} %gather_fusion.1), channel_id=2, replica_groups=mesh['groups'=2,'row'=4,'col'=4] {'row'}, dimensions={0}, use_global_device_ids=true | all-gather | bytes 163840 | tf_op jit(solution)/shard_map/all_gather | solution.py:106
  94.0 5.6 %all-gather.1 = bf16[64,8,128]{2,1,0:T(8,128)(2,1)S(1)} all-gather(bf16[16,8,128]{2,1,0:T(8,128)(2,1)S(1)} %gather_fusion.1), channel_id=3, replica_groups=mesh['groups'=2,'row'=4,'col'=4] {'col'}, dimensions={0}, use_global_device_ids=true | all-gather | bytes 163840 | tf_op jit(solution)/shard_map/all_gather | solution.py:99
  99.6 0.2 copy.19
  99.8 0.1 reshape.226
  100.0 0.4 copy.20
  100.4 0.5 fusion.44
  100.8 3.1 %copy.21 = f32[64,64,64]{0,1,2:T(8,128)} copy(f32[64,64,64]{2,1,0:T(8,128)S(1)} %fusion.44) | data formatting | bytes 2097152 | tf_op jit(solution)/shard_map/ikb,jkb->ijb/dot_general | solution.py:113
  103.9 0.5 fusion.48
  104.4 3.1 %copy.22 = f32[64,64,64]{0,1,2:T(8,128)} copy(f32[64,64,64]{2,1,0:T(8,128)S(1)} %fusion.48) | data formatting | bytes 2097152 | tf_op jit(solution)/shard_map/ikb,jkb->ijb/dot_general | solution.py:114
  107.5 3.8 %fusion.2 = bf16[64,1,64,128]{3,2,1,0:T(8,128)(2,1)} fusion(f32[64,1,64,64]{3,2,1,0:T(8,128)} %bitcast.114, f32[64,1,64,64]{3,2,1,0:T(8,128)} %bitcast.113), kind=kLoop, calls=%fused_computation.10 | loop fusion | flops 1572864 | bytes 3145728 | tf_op jit(solution)/shard_map/convert_element_type | solution.py:115
  (13 shorter events, 0.1 us)
Async XLA Ops:
  3.0 66.3 %all-to-all-start.1 = ((bf16[4,1,4]{2,1,0:T(2,128)(2,1)}), bf16[4,1,4]{2,1,0:T(2,128)(2,1)S(1)}, u32[]{:S(2)}, u32[]{:S(2)}) async-start(bf16[4,1,4]{2,1,0:T(2,128)(2,1)} %convert_element_type.76), calls=%async_computation.1 | async-start | bytes 4096 | tf_op jit(solution)/shard_map/all_to_all | solution.py:94
  41.4 22.4 %copy-start = (s32[64]{0:T(128)S(1)}, s32[64]{0:T(128)}, u32[]{:S(2)}) copy-start(s32[64]{0:T(128)} %param.9) | copy-start | bytes 772
  69.3 10.8 %all-to-all-start = ((bf16[4,4,8,128]{3,2,1,0:T(8,128)(2,1)}), bf16[4,4,8,128]{3,2,1,0:T(8,128)(2,1)S(1)}, u32[]{:S(2)}, u32[]{:S(2)}) async-start(bf16[4,4,8,128]{3,2,1,0:T(8,128)(2,1)} %broadcast_select_fusion), calls=%async_computation | async-start | bytes 65536 | tf_op jit(solution)/shard_map/all_to_all | solution.py:93
where the time goes:
time: 112 us; the launch traced here: 111 us
  matrix products  45.6 us (41%)
  local copies, waits for them, and re-layouts  19 us (17%)
  blocking collectives  18.9 us (17%)
  starting transfers between devices  11.4 us (10%)
  other arithmetic  10.1 us (9%)
  waiting for transfers between devices  5.41 us (5%)
    dot_general x1, matrix products, decimate(): jnp.einsum('iqbw,wn->iqbn', window, lower, preferred_element_type=jnp.flo...  22.2 us
    dot_general x1, matrix products, decimate(): jnp.einsum('iqbw,wn->iqbn', window, upper, preferred_element_type=jnp.flo...  22 us
    all_gather x1, blocking collectives, on_device(): piece = lax.all_gather(white_own, 'row', axis=0, tiled=True)  13.3 us
    all_to_all x1, starting transfers between devices, on_device(): lax.all_to_all(labels, 'row', split_axis=0, concat_axis=0, tiled=True)  6.35 us
    all_gather x1, blocking collectives, on_device(): row_white = lax.all_gather(white_own, 'col', axis=0, tiled=True)  5.58 us
    all_to_all x1, waiting for transfers between devices, on_device(): lax.all_to_all(outgoing, 'row', split_axis=0, concat_axis=0, tiled=True)  5.41 us
    all_to_all x1, starting transfers between devices, on_device(): lax.all_to_all(outgoing, 'row', split_axis=0, concat_axis=0, tiled=True)  5.09 us
    slice x2, local copies, waits for them, and re-layouts, decimate(): fir_taps[index]  3.9 us
  transfers between devices with their start and end apart: 2, of which 1 were waited for; matrix products, arithmetic and copies ran while one was open for 54% of the time, Pallas kernels for 0%

commit v1 on v0

--- a/solution.py
+++ b/solution.py
@@ -6,6 +6,28 @@
 
 CH_DEV = 16
 DEC = 4
+
+
+def cut_along(value, dim, length):
+    before, after = (value.shape[:dim], value.shape[dim + 1 :])
+    return jnp.moveaxis(value.reshape(*before, length, -1, *after), dim, 0)
+
+
+def joined_along(blocks, dim):
+    lengths = list(blocks.shape[1:])
+    lengths[dim] *= blocks.shape[0]
+    return jnp.moveaxis(blocks, 0, dim).reshape(lengths)
+
+
+def pairwise_exchange(shard, axis, split_dim, concat_dim):
+    size, place = (lax.axis_size(axis), lax.axis_index(axis))
+    parts = cut_along(shard, split_dim, size)
+    outs = [parts[place]]
+    for step in range(1, size):
+        sent = parts[place ^ step]
+        outs.append(lax.ppermute(sent, axis, [(i, i ^ step) for i in range(size)]))
+    parts = jnp.stack(outs)[place ^ jnp.arange(size)]
+    return joined_along(parts, concat_dim)
 
 
 def decimate(signal, fir_taps):
@@ -91,7 +113,7 @@
     outgoing = pack(reader_white, source, filled, nrows, capacity)
     arrived, arrived_labels = (
         lax.all_to_all(outgoing, "row", split_axis=0, concat_axis=0, tiled=True),
-        lax.all_to_all(labels, "row", split_axis=0, concat_axis=0, tiled=True),
+        pairwise_exchange(labels, "row", 0, 0),
     )
     white_own = settle(arrived, arrived_labels)
     records = white_own.shape[1]

time: 112 us -> 112 us (level)
    all_to_all x1 -> x0, starting transfers between devices: 6.35 us -> none  [on_device(): lax.all_to_all(labels, 'row', split_axis=0, concat_axis=0, tiled=True)]
    all_to_all x1, waiting for transfers between devices: 5.41 us -> 0.01 us  [on_device(): lax.all_to_all(outgoing, 'row', split_axis=0, concat_axis=0, tiled=True)]
    ppermute x0 -> x3, waiting for transfers between devices: none -> 5.27 us  [pairwise_exchange(): outs.append(lax.ppermute(sent, axis, [(i, i ^ step) for i in range(size)]))]
    ppermute x0 -> x3, starting transfers between devices: none -> 4.53 us  [pairwise_exchange(): outs.append(lax.ppermute(sent, axis, [(i, i ^ step) for i in range(size)]))]
    all_to_all x1, starting transfers between devices: 5.09 us -> 6.35 us  [on_device(): lax.all_to_all(outgoing, 'row', split_axis=0, concat_axis=0, tiled=True)]
    another operation x1 -> x2, other arithmetic: 3.59 us -> 3.6 us
    unnamed x4 -> x5, local copies, waits for them, and re-layouts: 2.56 us -> 2.56 us
  transfers between devices with their start and end apart: 2 -> 4, of which waited for: 1 -> 2; matrix products, arithmetic and copies ran while one was open for 54% -> 1% of each run, Pallas kernels for 0% -> 0%
where the time goes in v1:
time: 112 us; the launch traced here: 111 us
  matrix products  45.8 us (41%)
  local copies, waits for them, and re-layouts  19 us (17%)
  blocking collectives  19 us (17%)
  starting transfers between devices  10.9 us (10%)
  other arithmetic  10.1 us (9%)
  waiting for transfers between devices  5.27 us (5%)
    dot_general x1, matrix products, decimate(): jnp.einsum('iqbw,wn->iqbn', window, lower, preferred_element_type=jnp.flo...  22.3 us
    dot_general x1, matrix products, decimate(): jnp.einsum('iqbw,wn->iqbn', window, upper, preferred_element_type=jnp.flo...  22.1 us
    all_gather x1, blocking collectives, on_device(): piece = lax.all_gather(white_own, 'row', axis=0, tiled=True)  13.4 us
    all_to_all x1, starting transfers between devices, on_device(): lax.all_to_all(outgoing, 'row', split_axis=0, concat_axis=0, tiled=True)  6.35 us
    all_gather x1, blocking collectives, on_device(): row_white = lax.all_gather(white_own, 'col', axis=0, tiled=True)  5.58 us
    ppermute x3, waiting for transfers between devices, pairwise_exchange(): outs.append(lax.ppermute(sent, axis, [(i, i ^ step) for i in range(size)]))  5.27 us
    ppermute x3, starting transfers between devices, pairwise_exchange(): outs.append(lax.ppermute(sent, axis, [(i, i ^ step) for i in range(size)]))  4.53 us
    slice x2, local copies, waits for them, and re-layouts, decimate(): fir_taps[index]  3.91 us
  transfers between devices with their start and end apart: 4, of which 2 were waited for; matrix products, arithmetic and copies ran while one was open for 1% of the time, Pallas kernels for 0%

profile of v1, /device:TPU:0, one launch (start us, length us, event | category | flops | bytes accessed | tf_op | source)
XLA Modules:
  0.0 110.9 jit_solution(12567943602557087947)
XLA Ops:
  0.0 2.1 %fusion.139 = (f32[1]{0:T(128)}, f32[1]{0:T(128)}, f32[1]{0:T(128)}, f32[1]{0:T(128)}, f32[1]{0:T(128)}, /*index=5*/f32[1]{0:T(128)}, f32[1]{0:T(128)}, f32[1]{0...) fusion(f32[32]{0:T(128)} %param.8), kind=kLoop, calls=%fused_computation.196 | loop fusion | bytes 152 | tf_op jit(solution)/shard_map/slice | solution.py:50
  2.1 1.8 %fusion.140 = (f32[1]{0:T(128)}, f32[1]{0:T(128)}, f32[1]{0:T(128)}, f32[1]{0:T(128)}, f32[1]{0:T(128)}, /*index=5*/f32[1]{0:T(128)}, f32[1]{0:T(128)}, f32[1]{0...) fusion(f32[32]{0:T(128)} %param.8), kind=kLoop, calls=%fused_computation.197 | loop fusion | bytes 104 | tf_op jit(solution)/shard_map/slice | solution.py:50
  3.9 0.7 and_select_fusion.2
  4.6 0.7 fusion.68
  5.3 3.2 %pad_slice_fusion.1 = (bf16[16,8,12288]{2,1,0:T(8,128)(2,1)S(1)}, bf16[16,8,12288]{2,1,0:T(8,128)(2,1)S(1)}) fusion(bf16[16,8,12000]{2,1,0:T(8,128)(2,1)} %bitcast.125), kind=kLoop, calls=%fused_computation.7 | loop fusion | bytes 9363456 | tf_op jit(solution)/shard_map/slice | solution.py:42
  8.5 1.3 %copy.28 = bf16[16,8,24,512]{3,2,1,0:T(8,128)(2,1)S(1)} copy(bf16[16,8,24,512]{3,1,2,0:T(8,128)(2,1)S(1)} %bitcast.122) | data formatting | bytes 6291456
  9.7 0.1 slice.159
  9.9 1.3 %copy.29 = bf16[16,8,24,512]{3,2,1,0:T(8,128)(2,1)S(1)} copy(bf16[16,8,24,512]{3,1,2,0:T(8,128)(2,1)S(1)} %bitcast.121) | data formatting | bytes 6291456
  11.2 22.3 %fusion = f32[16,8,24,128]{3,2,1,0:T(8,128)S(1)} fusion(bf16[16,8,24,28]{3,2,1,0:T(8,128)(2,1)S(1)} %slice.159, bf16[16,8,24,512]{3,2,1,0:T(8,128)(2,1)S(1)} %copy.29, f32[]{:T(128)} %bitcast.35, f32[]{:T(128)} %bitcast.34, f32[]{:T(128)} %bitcast.33, f32[]{:T(128)} %bitcast.32, f32[]{:T(128)} %bitcast.31, f32[]{:T(128)} %bitcast.30, f32[]{:T(128)} %bitcast.29, ...), kind=kOutput, calls=%fused_computation.8 | convolution fusion | flops 438220800 | bytes 4891264 | tf_op jit(solution)/shard_map/iqbw,wn->iqbn/dot_general | solution.py:54
  33.4 0.0 copy-start
  33.4 22.1 %add_convert_fusion = bf16[16,8,24,128]{3,2,1,0:T(8,128)(2,1)S(1)} fusion(f32[16,8,24,128]{3,2,1,0:T(8,128)S(1)} %fusion, bf16[16,8,24,28]{3,2,1,0:T(8,128)(2,1)S(1)} %slice.159, bf16[16,8,24,512]{3,2,1,0:T(8,128)(2,1)S(1)} %copy.29, f32[]{:T(128)} %bitcast.35, f32[]{:T(128)} %bitcast.34, f32[]{:T(128)} %bitcast.33, f32[]{:T(128)} %bitcast.32, ...), kind=kOutput, calls=%fused_computation.12 | convolution fusion | flops 438799872 | bytes 5677696 | tf_op jit(solution)/shard_map/iqbw,wn->iqbn/dot_general | solution.py:53
  55.5 0.3 reshape.214
  55.9 0.0 copy-done
  55.9 3.6 %cosine_convert_fusion = (bf16[3000,64]{0,1:T(8,128)(2,1)S(1)}, bf16[3000,64]{0,1:T(8,128)(2,1)S(1)}) fusion(s32[64]{0:T(128)S(1)} %copy-done), kind=kLoop, calls=%fused_computation.22 | loop fusion | flops 2304000 | bytes 768256 | tf_op jit(solution)/shard_map/convert.1
  59.5 0.5 multiply_reduce_fusion
  60.6 0.2 convert_reduce_fusion.1
  60.8 0.1 select_reduce_fusion.1
  61.0 0.1 gt.12
  61.1 0.1 fusion.60
  61.2 0.6 gather_fusion
  61.7 0.7 broadcast_select_fusion
  62.5 6.4 %all-to-all-start = ((bf16[4,4,8,128]{3,2,1,0:T(8,128)(2,1)}), bf16[4,4,8,128]{3,2,1,0:T(8,128)(2,1)S(1)}, u32[]{:S(2)}, u32[]{:S(2)}) async-start(bf16[4,4,8,128]{3,2,1,0:T(8,128)(2,1)} %broadcast_select_fusion), calls=%async_computation | async-start | bytes 65536 | tf_op jit(solution)/shard_map/all_to_all | solution.py:115
  68.8 0.1 reduce_sum.66
  68.9 2.1 %collective-permute-start = (bf16[1,4]{1,0:T(2,128)(2,1)S(1)}, bf16[1,4]{1,0:T(2,128)(2,1)S(1)}, u32[]{:S(2)}, u32[]{:S(2)}) collective-permute-start(bf16[1,4]{1,0:T(2,128)(2,1)S(1)} %get-tuple-element.15), channel_id=1, source_target_pairs={{0,4},{4,0},{8,12},{12,8},{1,5},{5,1},{9,13},{13,9},{2,6},{6,2},{1... | collective-permute-start | bytes 32 | tf_op jit(solution)/shard_map/ppermute | solution.py:28
  71.0 2.4 %collective-permute-start.1 = (bf16[1,4]{1,0:T(2,128)(2,1)S(1)}, bf16[1,4]{1,0:T(2,128)(2,1)S(1)}, u32[]{:S(2)}, u32[]{:S(2)}) collective-permute-start(bf16[1,4]{1,0:T(2,128)(2,1)S(1)} %get-tuple-element.14), channel_id=1, source_target_pairs={{0,8},{4,12},{8,0},{12,4},{1,9},{5,13},{9,1},{13,5},{2,10},{6,14},... | collective-permute-start | bytes 32 | tf_op jit(solution)/shard_map/ppermute | solution.py:28
  73.4 0.1 collective-permute-start.2
  73.5 0.0 collective-permute-done
  73.5 2.0 %collective-permute-done.1 = bf16[1,4]{1,0:T(2,128)(2,1)S(1)} collective-permute-done((bf16[1,4]{1,0:T(2,128)(2,1)S(1)}, bf16[1,4]{1,0:T(2,128)(2,1)S(1)}, u32[]{:S(2)}, u32[]{:S(2)}) %collective-permute-start.1) | collective-permute-done | bytes 40 | tf_op jit(solution)/shard_map/ppermute | solution.py:28
  75.5 3.3 %collective-permute-done.2 = bf16[1,4]{1,0:T(2,128)(2,1)S(1)} collective-permute-done((bf16[1,4]{1,0:T(2,128)(2,1)S(1)}, bf16[1,4]{1,0:T(2,128)(2,1)S(1)}, u32[]{:S(2)}, u32[]{:S(2)}) %collective-permute-start.2) | collective-permute-done | bytes 40 | tf_op jit(solution)/shard_map/ppermute | solution.py:28
  78.8 0.6 gather_fusion.1
  79.3 0.1 reshape.220
  79.4 0.1 select_reduce_fusion
  79.6 0.0 all-to-all-done
  79.6 0.6 gather_fusion.2
  80.1 13.4 %all-gather = bf16[64,8,128]{2,1,0:T(8,128)(2,1)S(1)} all-gather(bf16[16,8,128]{2,1,0:T(8,128)(2,1)S(1)} %gather_fusion.2), channel_id=2, replica_groups=mesh['groups'=2,'row'=4,'col'=4] {'row'}, dimensions={0}, use_global_device_ids=true | all-gather | bytes 163840 | tf_op jit(solution)/shard_map/all_gather | solution.py:128
  93.6 5.6 %all-gather.1 = bf16[64,8,128]{2,1,0:T(8,128)(2,1)S(1)} all-gather(bf16[16,8,128]{2,1,0:T(8,128)(2,1)S(1)} %gather_fusion.2), channel_id=3, replica_groups=mesh['groups'=2,'row'=4,'col'=4] {'col'}, dimensions={0}, use_global_device_ids=true | all-gather | bytes 163840 | tf_op jit(solution)/shard_map/all_gather | solution.py:121
  99.2 0.2 copy.16
  99.4 0.1 reshape.218
  99.6 0.4 copy.17
  100.0 0.5 fusion.44
  100.4 3.1 %copy.18 = f32[64,64,64]{0,1,2:T(8,128)} copy(f32[64,64,64]{2,1,0:T(8,128)S(1)} %fusion.44) | data formatting | bytes 2097152 | tf_op jit(solution)/shard_map/ikb,jkb->ijb/dot_general | solution.py:135
  103.5 0.5 fusion.48
  104.0 3.1 %copy.19 = f32[64,64,64]{0,1,2:T(8,128)} copy(f32[64,64,64]{2,1,0:T(8,128)S(1)} %fusion.48) | data formatting | bytes 2097152 | tf_op jit(solution)/shard_map/ikb,jkb->ijb/dot_general | solution.py:136
  107.1 3.8 %fusion.2 = bf16[64,1,64,128]{3,2,1,0:T(8,128)(2,1)} fusion(f32[64,1,64,64]{3,2,1,0:T(8,128)} %bitcast.124, f32[64,1,64,64]{3,2,1,0:T(8,128)} %bitcast.123), kind=kLoop, calls=%fused_computation.11 | loop fusion | flops 1572864 | bytes 3145728 | tf_op jit(solution)/shard_map/convert_element_type | solution.py:137
  (18 shorter events, 0.2 us)
Async XLA Ops:
  33.4 22.4 %copy-start = (s32[64]{0:T(128)S(1)}, s32[64]{0:T(128)}, u32[]{:S(2)}) copy-start(s32[64]{0:T(128)} %param.9) | copy-start | bytes 772
  62.5 17.1 %all-to-all-start = ((bf16[4,4,8,128]{3,2,1,0:T(8,128)(2,1)}), bf16[4,4,8,128]{3,2,1,0:T(8,128)(2,1)S(1)}, u32[]{:S(2)}, u32[]{:S(2)}) async-start(bf16[4,4,8,128]{3,2,1,0:T(8,128)(2,1)} %broadcast_select_fusion), calls=%async_computation | async-start | bytes 65536 | tf_op jit(solution)/shard_map/all_to_all | solution.py:115
  68.9 4.5 %collective-permute-start = (bf16[1,4]{1,0:T(2,128)(2,1)S(1)}, bf16[1,4]{1,0:T(2,128)(2,1)S(1)}, u32[]{:S(2)}, u32[]{:S(2)}) collective-permute-start(bf16[1,4]{1,0:T(2,128)(2,1)S(1)} %get-tuple-element.15), channel_id=1, source_target_pairs={{0,4},{4,0},{8,12},{12,8},{1,5},{5,1},{9,13},{13,9},{2,6},{6,2},{1... | collective-permute-start | bytes 32 | tf_op jit(solution)/shard_map/ppermute | solution.py:28
  71.0 4.5 %collective-permute-start.1 = (bf16[1,4]{1,0:T(2,128)(2,1)S(1)}, bf16[1,4]{1,0:T(2,128)(2,1)S(1)}, u32[]{:S(2)}, u32[]{:S(2)}) collective-permute-start(bf16[1,4]{1,0:T(2,128)(2,1)S(1)} %get-tuple-element.14), channel_id=1, source_target_pairs={{0,8},{4,12},{8,0},{12,4},{1,9},{5,13},{9,1},{13,5},{2,10},{6,14},... | collective-permute-start | bytes 32 | tf_op jit(solution)/shard_map/ppermute | solution.py:28
  73.4 5.4 %collective-permute-start.2 = (bf16[1,4]{1,0:T(2,128)(2,1)S(1)}, bf16[1,4]{1,0:T(2,128)(2,1)S(1)}, u32[]{:S(2)}, u32[]{:S(2)}) collective-permute-start(bf16[1,4]{1,0:T(2,128)(2,1)S(1)} %get-tuple-element.13), channel_id=1, source_target_pairs={{0,12},{4,8},{8,4},{12,0},{1,13},{5,9},{9,5},{13,1},{2,14},{6,10},... | collective-permute-start | bytes 32 | tf_op jit(solution)/shard_map/ppermute | solution.py:28
